TPU v7x, 128 devices: a whole 4x4x4 slice. The times are simulated.
128 devices in a mesh: rows: 8 (over y, x_hi), cols: 16 (over x_lo, z, core).
Axes of the slice: x: 4 (x_hi: 2, x_lo: 2; x = x_hi * 2 + x_lo), y: 4, z: 4, core: 2. Of those that a mesh axis runs over, the one named last changes fastest.
Arguments:
- object_field: float32 [2, 2048, 4096], P(None, 'rows', 'cols'), may hold values from -6 to 6
- probe: float32 [2, 256, 256], replicated, may hold values from -6 to 6
- positions: int32 [8, 16, 6, 2], P('rows', 'cols'), may hold values from 0 to 256
- counts: int32 [8, 16], P('rows', 'cols'), may hold values from 2 to 6
- intensity: int32 [8, 16, 6, 256, 256], P('rows', 'cols'), may hold values from 0 to 4000
Outputs:
- updated_field: float32 [2, 2048, 4096], P(None, 'rows', 'cols')
Inputs may be any that keep to these rules, and one draw needn't show every extreme that they name: Only the first counts[a, b] entries of tile (a, b) in positions and intensity are used.
All inputs are finite; a program needn't handle non-finite values.
Results may differ from a plain program's by a relative error of at most 0.00029.
Values sent between devices are 32-bit elements; how exact they have to be, the bound alone decides.
No kernel may reach another device: no remote copies, remote signals or barrier semaphores. Data moves between devices by JAX's collectives and lax.ppermute only.
A program may use at most 64 MiB of HBM per device.

v0:
```python
import functools

import jax
import jax.numpy as jnp
import numpy as np
from jax import lax
from jax.experimental import pallas as pl
from jax.experimental.pallas import tpu as pltpu
from jax.sharding import PartitionSpec as P

MARGIN = 128
HALF = 128
GROUP = 2


step_rate = 0.02
photon_unit = 0.001


def rotation_tables(length):
    half = length // 2
    index = np.arange(half, dtype=np.int64)
    angle = (index[:, None] * index[None, :] % half) * (2.0 * np.pi / half)
    norm = 1.0 / np.sqrt(length)
    cosine = np.cos(angle) * norm
    sine = np.sin(angle) * norm
    mixed = np.block([[cosine, -sine], [sine, cosine]]).astype(np.float32)
    turn = index * (2.0 * np.pi / length)
    twiddle = np.stack([np.cos(turn), -np.sin(turn)]).astype(np.float32)
    return mixed, twiddle


def split_order(length):
    half = length // 2
    order = np.concatenate([np.arange(half) * 2, np.arange(half) * 2 + 1])
    return (np.arange(length)[:, None] == order[None, :]).astype(np.float32)


VMEM = pl.BlockSpec(memory_space=pltpu.VMEM)
SMEM = pl.BlockSpec(memory_space=pltpu.SMEM)


def shaped(*dims):
    return jax.ShapeDtypeStruct(dims, jnp.float32)


def whole(body, outs, scalars, arrays, scratch=(), limit=40 << 20, flops=1 << 20):
    return pl.pallas_call(
        body,
        out_shape=outs,
        in_specs=[SMEM] * len(scalars) + [VMEM] * len(arrays),
        out_specs=tuple(VMEM for _ in outs),
        scratch_shapes=scratch,
        compiler_params=pltpu.CompilerParams(vmem_limit_bytes=limit),
        cost_estimate=pl.CostEstimate(flops=flops, bytes_accessed=8 << 20, transcendentals=0),
    )(*scalars, *arrays)


def split_columns(odd_col, tile, side_a, side_b):
    size = tile.shape[2]
    left, right = slice(0, MARGIN), slice(size - MARGIN, size)

    @pl.when(odd_col == 1)
    def _():
        side_a[...] = tile[:, :, left]
        side_b[...] = tile[:, :, right]

    @pl.when(odd_col == 0)
    def _():
        side_a[...] = tile[:, :, right]
        side_b[...] = tile[:, :, left]


def cut_rows_body(info, tile, edge_a, edge_b):
    edge = tile.shape[1] - MARGIN
    edge_a[...] = tile[:, pl.ds(pl.multiple_of((1 - info[0]) * edge, 8), MARGIN), :]
    edge_b[...] = tile[:, pl.ds(pl.multiple_of(info[0] * edge, 8), MARGIN), :]


def prepare_body(
    info, positions, intensity, probe, order, tile, measured, rolled, edge_a, edge_b, held, arrived
):
    slots, size = intensity.shape[0], probe.shape[1]
    half = size // 2
    moves = [order[:half], order[half:]]
    copies = [
        pltpu.make_async_copy(intensity.at[:, :, pl.ds(half * block, half)], held.at[block], arrived.at[block])
        for block in range(2)
    ]
    for copy in copies:
        copy.start()
    split_columns(info[1], tile, edge_a, edge_b)

    def turn(slot, carry):
        shift = lax.rem(positions[slot, 1], size)
        for part in range(2):
            rolled[slot, part] = pltpu.roll(probe[part], shift, 1)
        return carry

    lax.fori_loop(0, slots, turn, 0)
    for copy in copies:
        copy.wait()

    def reorder(slot, carry):
        for parity in range(2):
            moved = jnp.zeros((half, size), jnp.float32)
            for block in range(2):
                counts = held[block, slot, pl.ds(parity, half, stride=2), :]
                upper = lax.shift_right_logical(counts, 8).astype(jnp.float32).astype(jnp.bfloat16)
                lower = lax.bitwise_and(counts, 255).astype(jnp.float32).astype(jnp.bfloat16)
                high = jnp.dot(upper, moves[block], preferred_element_type=jnp.float32)
                low = jnp.dot(lower, moves[block], preferred_element_type=jnp.float32)
                moved = moved + (256.0 * high + low)
            measured[slot, parity] = moved * photon_unit
        return carry

    lax.fori_loop(0, slots, reorder, 0)


def prepare(info, positions, intensity, probe, order, tile):
    slots, size = intensity.shape[0], probe.shape[1]
    edge = shaped(2, tile.shape[1], MARGIN)
    half = size // 2
    return pl.pallas_call(
        prepare_body,
        out_shape=(shaped(slots, 2, half, size), shaped(slots, 2, size, size), edge, edge),
        in_specs=[SMEM, SMEM, pl.BlockSpec(memory_space=pl.ANY), VMEM, VMEM, VMEM],
        out_specs=(VMEM,) * 4,
        scratch_shapes=[pltpu.VMEM((2, slots, size, half), jnp.int32), pltpu.SemaphoreType.DMA((2,))],
        compiler_params=pltpu.CompilerParams(vmem_limit_bytes=24 << 20),
        cost_estimate=pl.CostEstimate(flops=slots * 2**27, bytes_accessed=8 << 20, transcendentals=0),
    )(info, positions, intensity, probe, order, tile)


def halves(value):
    upper = value.astype(jnp.bfloat16)
    lower = (value - upper.astype(jnp.float32)).astype(jnp.bfloat16)
    return upper, lower


def times_table(value, table):
    upper, lower = halves(value)
    packed = jnp.concatenate([upper, lower, upper], axis=1)
    return jnp.dot(packed, table, preferred_element_type=jnp.float32)


def table_times(table, value):
    upper, lower = halves(value)
    packed = jnp.concatenate([upper, lower, upper], axis=0)
    return jnp.dot(table, packed, preferred_element_type=jnp.float32)


def wide(left, right):
    return jnp.concatenate([left, right], axis=1)


def tall(upper, lower):
    return jnp.concatenate([upper, lower], axis=0)


def places(odd_col):
    return 3 - 3 * odd_col, 2 - odd_col, 1 + odd_col, 3 * odd_col


def gradient_body(first, info, positions, counts, ext_r, ext_i, ext_b, *refs):
    if first:
        near_edge, near_corner, far_edge, far_corner, *refs = refs
    else:
        near_r, near_i, far_strip, *refs = refs
    measured, rolled, fore_lane, fore_row, back_row, back_lane, twist_lane, twist_row, *refs = refs
    *outs, in_a, in_b, field, sums = refs
    size = rolled.shape[2]
    half = size // 2
    extent = field.shape[2]
    odd_col = info[1]
    other = 1 - odd_col
    near_at, a_at, b_at, far_at = places(odd_col)
    lanes = lax.broadcasted_iota(jnp.int32, (1, half), 1)
    sums[...] = jnp.zeros_like(sums)
    field[a_at, 0] = ext_r[...]
    field[a_at, 1] = ext_i[...]
    field[b_at] = ext_b[...]
    upper, middle, lower = slice(0, MARGIN), slice(MARGIN, extent - MARGIN), slice(extent - MARGIN, extent)
    if first:
        field[near_at, :, middle] = near_edge[other]
        field[near_at, :, upper] = near_corner[other, 0]
        field[near_at, :, lower] = near_corner[other, 1]
        field[far_at, :, middle] = far_edge[...]
        field[far_at, :, upper] = far_corner[0]
        field[far_at, :, lower] = far_corner[1]
    else:
        field[near_at, 0] = near_r[other]
        field[near_at, 1] = near_i[other]
        field[far_at] = far_strip[...]
    lane_r, lane_i = twist_lane[0], twist_lane[1]
    row_r, row_i = twist_row[0], twist_row[1]

    def enter(slot):
        rows = pl.ds(positions[slot, 0], size)
        waves = []
        for block in range(2):
            near = lanes + half * block >= positions[slot, 1]
            cut = slice(half * block, half * (block + 1))
            p_r, p_i = rolled[slot, 0, :, cut], rolled[slot, 1, :, cut]
            o_r = jnp.where(near, field[block, 0, rows, :], field[block + 2, 0, rows, :])
            o_i = jnp.where(near, field[block, 1, rows, :], field[block + 2, 1, rows, :])
            waves.append((p_r * o_r - p_i * o_i, p_r * o_i + p_i * o_r))
        (r0, i0), (r1, i1) = waves
        d_r, d_i = r0 - r1, i0 - i1
        return [
            wide(r0 + r1, i0 + i1),
            wide(d_r * lane_r - d_i * lane_i, d_r * lane_i + d_i * lane_r),
        ]

    def cross(pair):
        even, odd = pair
        r_all = wide(even[:, :half], odd[:, :half])
        i_all = wide(even[:, half:], odd[:, half:])
        r0, r1 = r_all[:half], r_all[half:]
        i0, i1 = i_all[:half], i_all[half:]
        d_r, d_i = r0 - r1, i0 - i1
        return [
            tall(r0 + r1, i0 + i1),
            tall(d_r * row_r - d_i * row_i, d_r * row_i + d_i * row_r),
        ]

    def scale(slot, pair):
        scaled = []
        for parity, spectrum in enumerate(pair):
            s_r, s_i = spectrum[:half], spectrum[half:]
            misfit = s_r * s_r + s_i * s_i - measured[slot, parity]
            scaled.append(tall(misfit * s_r, misfit * s_i))
        return scaled

    def cross_back(pair):
        even, odd = pair
        e_r, e_i = even[:half], even[half:]
        o_r, o_i = odd[:half], odd[half:]
        t_r = o_r * row_r + o_i * row_i
        t_i = o_i * row_r - o_r * row_i
        full_r = tall(e_r + t_r, e_r - t_r)
        full_i = tall(e_i + t_i, e_i - t_i)
        return [
            wide(full_r[:, :half], full_i[:, :half]),
            wide(full_r[:, half:], full_i[:, half:]),
        ]

    def leave(slot, pair, keep):
        rows = pl.ds(positions[slot, 0], size)
        even, odd = pair
        e_r, e_i = even[:, :half], even[:, half:]
        o_r, o_i = odd[:, :half], odd[:, half:]
        t_r = o_r * lane_r + o_i * lane_i
        t_i = o_i * lane_r - o_r * lane_i
        outs = [(e_r + t_r, e_i + t_i), (e_r - t_r, e_i - t_i)]
        for block, (b_r, b_i) in enumerate(outs):
            place = lanes + half * block
            near = place >= positions[slot, 1]
            far = place < positions[slot, 1]
            if keep is not None:
                near, far = near & keep, far & keep
            cut = slice(half * block, half * (block + 1))
            p_r, p_i = rolled[slot, 0, :, cut], rolled[slot, 1, :, cut]
            terms = (p_r * b_r + p_i * b_i, p_r * b_i - p_i * b_r)
            for part, term in enumerate(terms):
                sums[block, part, rows, :] += jnp.where(near, term, 0.0)
                sums[block + 2, part, rows, :] += jnp.where(far, term, 0.0)

    def one_group(group, carry):
        slots = [GROUP * group + i for i in range(GROUP)]
        live = [None] + [slot < counts[0, 0] for slot in slots[1:]]
        pairs = [enter(slot) for slot in slots]
        pairs = [[times_table(half_, fore_lane[...]) for half_ in pair] for pair in pairs]
        pairs = [cross(pair) for pair in pairs]
        pairs = [[table_times(fore_row[...], half_) for half_ in pair] for pair in pairs]
        pairs = [scale(slot, pair) for slot, pair in zip(slots, pairs)]
        pairs = [[table_times(back_row[...], half_) for half_ in pair] for pair in pairs]
        pairs = [cross_back(pair) for pair in pairs]
        pairs = [[times_table(half_, back_lane[...]) for half_ in pair] for pair in pairs]
        for slot, pair, keep in zip(slots, pairs, live):
            leave(slot, pair, keep)
        return carry

    lax.fori_loop(0, (counts[0, 0] + GROUP - 1) // GROUP, one_group, 0)
    if first:
        out_r, out_i, out_b = outs
        out_r[...] = sums[near_at, 0]
        out_i[...] = sums[near_at, 1]
        out_b[...] = sums[far_at]
    else:
        for at, corner, edge in ((near_at, *outs[:2]), (far_at, *outs[2:])):
            corner[0] = sums[at, :, upper]
            corner[1] = sums[at, :, lower]
            edge[...] = sums[at, :, middle]
    in_a[...] = sums[a_at]
    in_b[...] = sums[b_at]


def gradient(first, info, positions, counts, ext, sides, measured, rolled, tables):
    extent = ext[0].shape[0]
    plane, strip = shaped(extent, HALF), shaped(2, extent, HALF)
    corner, edge = shaped(2, 2, MARGIN, HALF), shaped(2, extent - 2 * MARGIN, HALF)
    outs = (plane, plane, strip) if first else (corner, edge, corner, edge)
    return whole(
        functools.partial(gradient_body, first),
        (*outs, strip, strip),
        (info, positions, counts),
        (*ext, *sides, measured, rolled, *tables),
        [pltpu.VMEM((4, 2, extent, HALF), jnp.float32)] * 2,
        flops=6 * 8 * 3 * 2**25,
    )


def extend_body(info, tile, halo_a, halo_b, ext_r, ext_i, ext_b, corner_a, corner_b):
    size = tile.shape[1]
    odd_row, odd_col = info[0], info[1]

    def fill(cut_a, cut_b):
        above = [jnp.where(odd_row == 1, halo_a[part], halo_b[part]) for part in range(2)]
        below = [jnp.where(odd_row == 1, halo_b[part], halo_a[part]) for part in range(2)]
        targets = [ext_r, ext_i]
        for part in range(2):
            corner_a[0, part] = above[part][:, cut_a]
            corner_a[1, part] = below[part][:, cut_a]
            corner_b[0, part] = above[part][:, cut_b]
            corner_b[1, part] = below[part][:, cut_b]
            targets[part][:MARGIN, :] = above[part][:, cut_a]
            targets[part][MARGIN : MARGIN + size, :] = tile[part, :, cut_a]
            targets[part][MARGIN + size :, :] = below[part][:, cut_a]
            ext_b[part, :MARGIN] = above[part][:, cut_b]
            ext_b[part, MARGIN : MARGIN + size] = tile[part, :, cut_b]
            ext_b[part, MARGIN + size :] = below[part][:, cut_b]

    left, right = slice(0, HALF), slice(HALF, 2 * HALF)

    @pl.when(odd_col == 1)
    def _():
        fill(left, right)

    @pl.when(odd_col == 0)
    def _():
        fill(right, left)


def outgoing(odd_row, total, width, out_a, out_b):
    extent = total.shape[1]
    out_a[...] = total[:, pl.ds(pl.multiple_of((1 - odd_row) * (extent - width), 8), width), :]
    out_b[...] = total[:, pl.ds(pl.multiple_of(odd_row * (extent - width), 8), width), :]


def join_near_body(info, inner, near_r, near_i, total, out_a, out_b):
    other = 1 - info[1]
    total[0] = inner[0] + near_r[other]
    total[1] = inner[1] + near_i[other]
    outgoing(info[0], total, total.shape[1] // 2, out_a, out_b)


def join_far_body(info, inner, strip, waiting, total, out_a, out_b, passed):
    total[...] = inner[...] + strip[...]
    outgoing(info[0], total, total.shape[1] // 2, out_a, out_b)
    passed[...] = waiting[...]


def corner_near_body(info, inner, corner, out_a, out_b):
    add_corner(info, inner, corner.at[1 - info[1]], out_a, out_b)


def corner_far_body(info, inner, corner, earlier, waiting, out_a, out_b, passed):
    add_corner(info, inner, corner, out_a, out_b)
    passed[...] = waiting[...]


def add_corner(info, inner, corner, out_a, out_b):
    last = inner.shape[1] - MARGIN
    lower, upper = 1 - info[0], info[0]
    out_a[...] = inner[:, pl.ds(pl.multiple_of(lower * last, 8), MARGIN), :] + corner[lower]
    out_b[...] = inner[:, pl.ds(pl.multiple_of(upper * last, 8), MARGIN), :] + corner[upper]


def updated(info, part, ext, total, halo_a, halo_b):
    middle = total.shape[1] // 2
    above = total[part, :middle] + jnp.where(info[0] == 1, halo_a[part], halo_b[part])
    below = total[part, middle:] + jnp.where(info[0] == 1, halo_b[part], halo_a[part])
    row = lax.broadcasted_iota(jnp.int32, (middle, HALF), 0)
    above = jnp.where((info[2] == 1) & (row < MARGIN), 0.0, above)
    below = jnp.where((info[3] == 1) & (row >= middle - MARGIN), 0.0, below)
    return tall(ext[:middle] - step_rate * above, ext[middle:] - step_rate * below)


def update_near_body(info, ext_r, ext_i, total, halo_a, halo_b, out_r, out_i):
    out_r[...] = updated(info, 0, ext_r, total, halo_a, halo_b)
    out_i[...] = updated(info, 1, ext_i, total, halo_a, halo_b)


def update_far_body(info, ext_b, total, halo_a, halo_b, out):
    for part in range(2):
        out[part] = updated(info, part, ext_b.at[part], total, halo_a, halo_b)


def finish_body(
    info, ext_r, ext_i, ext_b, inner_a, inner_b, edge_a, edge_b, near_a, near_b, far_a, far_b, out
):
    size = out.shape[1]
    half = size // 2
    upper, lower = slice(MARGIN, MARGIN + half), slice(MARGIN + half, MARGIN + size)

    def settle(cut, ext, inner, edge, halo_a, halo_b):
        for part in range(2):
            above = jnp.where(info[0] == 1, halo_a[part], halo_b[part])
            below = jnp.where(info[0] == 1, halo_b[part], halo_a[part])
            above = inner[part, upper] + edge[part, :half] + above
            below = inner[part, lower] + edge[part, half:] + below
            out[part, :half, cut] = ext[part][upper] - step_rate * above
            out[part, half:, cut] = ext[part][lower] - step_rate * below

    def place(cut_a, cut_b):
        settle(cut_a, [ext_r, ext_i], inner_a, edge_a.at[1 - info[1]], near_a, near_b)
        settle(cut_b, [ext_b.at[0], ext_b.at[1]], inner_b, edge_b, far_a, far_b)

    left, right = slice(0, HALF), slice(HALF, 2 * HALF)

    @pl.when(info[1] == 1)
    def _():
        place(left, right)

    @pl.when(info[1] == 0)
    def _():
        place(right, left)


def constants(size):
    half = size // 2
    mixed, twiddle = rotation_tables(size)
    upper = mixed.astype(jnp.bfloat16)
    lower = (mixed - upper.astype(np.float32)).astype(jnp.bfloat16)
    fore_lane = jnp.asarray(np.concatenate([upper, upper, lower], axis=0))
    back_row = jnp.asarray(np.concatenate([upper, upper, lower], axis=1))
    fore_row = jnp.asarray(np.concatenate([upper.T, upper.T, lower.T], axis=1))
    back_lane = jnp.asarray(np.concatenate([upper.T, upper.T, lower.T], axis=0))
    twist_lane = jnp.asarray(twiddle.reshape(2, 1, half))
    twist_row = jnp.asarray(np.ascontiguousarray(np.broadcast_to(twiddle[:, :, None], (2, half, size))))
    return fore_lane, fore_row, back_row, back_lane, twist_lane, twist_row


def swapped(value, axis, first):
    count = lax.axis_size(axis)
    route = []
    for i in range(first, count - 1, 2):
        route += [(i, i + 1), (i + 1, i)]
    return lax.ppermute(value, axis, route)


def paired(value):
    groups = [[i, i + 1] for i in range(0, lax.axis_size("cols"), 2)]
    return lax.all_gather(value, "cols", axis_index_groups=groups)


def both_rows(edge_a, edge_b):
    return swapped(edge_a, "rows", 0), swapped(edge_b, "rows", 1)


def on_device(object_field, probe, positions, counts, intensity):
    size = probe.shape[1]
    tile = object_field.shape[1]
    extent = tile + 2 * MARGIN
    row, col = lax.axis_index("rows"), lax.axis_index("cols")
    last = lax.axis_size("rows") - 1
    info = jnp.stack([row % 2, col % 2, row == 0, row == last]).astype(jnp.int32)
    tables = constants(size)
    order = jnp.asarray(split_order(size)).astype(jnp.bfloat16)
    positions, intensity = positions[0, 0], intensity[0, 0]
    plane, strip = shaped(extent, HALF), shaped(2, extent, HALF)
    corner = shaped(2, 2, MARGIN, HALF)

    edge = shaped(2, MARGIN, tile)
    halos = both_rows(*whole(cut_rows_body, (edge, edge), (info,), (object_field,)))
    measured, rolled, edge_a, edge_b = prepare(info, positions, intensity, probe, order, object_field)
    far_edge, near_edge = swapped(edge_b, "cols", 1), paired(edge_a)
    *ext, corner_a, corner_b = whole(
        extend_body, (plane, plane, strip, corner, corner), (info,), (object_field, *halos)
    )
    far_corner = swapped(corner_b, "cols", 1)
    sides = near_edge, paired(corner_a), far_edge, far_corner
    out_r, out_i, out_b, in_a, in_b = gradient(
        True, info, positions, counts, ext, sides, measured, rolled, tables
    )

    far = swapped(out_b, "cols", 1)
    near = paired(out_r), paired(out_i)
    piece = shaped(2, extent // 2, HALF)
    total_a, edge_a, edge_b = whole(join_near_body, (strip, piece, piece), (info,), (in_a, *near))
    near_halo_a = swapped(edge_a, "rows", 0)
    total_b, far_a, far_b, edge_b = whole(
        join_far_body, (strip, piece, piece, piece), (info,), (in_b, far, edge_b)
    )
    far_halos = both_rows(far_a, far_b)
    near_halos = near_halo_a, swapped(edge_b, "rows", 1)
    far_ext = whole(update_far_body, (strip,), (info,), (ext[2], total_b, *far_halos))
    near_ext = whole(update_near_body, (plane, plane), (info,), (*ext[:2], total_a, *near_halos))
    ext = (*near_ext, *far_ext)
    sides = paired(ext[0]), paired(ext[1]), swapped(ext[2], "cols", 1)
    corner_a, edge_a, corner_b, edge_b, in_a, in_b = gradient(
        False, info, positions, counts, ext, sides, measured, rolled, tables
    )

    piece = shaped(2, MARGIN, HALF)
    far_corner = swapped(corner_b, "cols", 1)
    near_corner = paired(corner_a)
    rows_a, rows_b = whole(corner_near_body, (piece, piece), (info,), (in_a, near_corner))
    near_halos = both_rows(rows_a, rows_b)
    edge = shaped(2, tile, HALF)
    far_a, far_b, edge_b = whole(
        corner_far_body, (piece, piece, edge), (info,), (in_b, far_corner, rows_b, edge_b)
    )
    far_halos = both_rows(far_a, far_b)
    sides = paired(edge_a), swapped(edge_b, "cols", 1)
    return whole(
        finish_body, (shaped(2, tile, tile),), (info,), (*ext, in_a, in_b, *sides, *near_halos, *far_halos)
    )[0]


def solution(mesh):
    placed = (
        P(None, "rows", "cols"),
        P(),
        P("rows", "cols", None, None),
        P("rows", "cols"),
        P("rows", "cols", None, None, None),
    )
    return jax.shard_map(
        on_device, mesh=mesh, in_specs=placed, out_specs=P(None, "rows", "cols"), check_vma=False
    )
```

profile of v0, /device:TPU:10, one launch (start us, length us, event | category | flops | bytes accessed | tf_op | source)
XLA Modules:
  0.0 125.3 jit_solution(15881916065859075654)
XLA Ops:
  1.7 2.2 %collective-permute-start = (f32[2,128,256]{2,1,0:T(8,128)S(1)}, f32[2,128,256]{2,1,0:T(8,128)S(1)}, u32[]{:S(2)}, u32[]{:S(2)}) collective-permute-start(f32[2,128,256]{2,1,0:T(8,128)S(1)} %get-tuple-element.41), channel_id=1, source_target_pairs={{0,16},{16,0},{32,48},{48,32},{64,80},{80,64},{96,112},{112,96},{1... | collective-permute-start | bytes 786440 | tf_op jit(solution)/shard_map/ppermute | solution.py:450
  3.9 3.2 %collective-permute-start.1 = (f32[2,128,256]{2,1,0:T(8,128)S(1)}, f32[2,128,256]{2,1,0:T(8,128)S(1)}, u32[]{:S(2)}, u32[]{:S(2)}) collective-permute-start(f32[2,128,256]{2,1,0:T(8,128)S(1)} %get-tuple-element.42), channel_id=1, source_target_pairs={{16,32},{32,16},{48,64},{64,48},{80,96},{96,80},{17,33},{33,17},{4... | collective-permute-start | bytes 786440 | tf_op jit(solution)/shard_map/ppermute | solution.py:450
  12.3 3.8 %shard_map.120 = (f32[6,2,128,256]{3,2,1,0:T(8,128)S(1)}, f32[6,2,256,256]{3,2,1,0:T(8,128)S(1)}, f32[2,256,128]{2,1,0:T(8,128)S(1)}, f32[2,256,128]{2,1,0:T(8,128)S(1)}) custom-call(s32[4]{0:T(128)S(1)} %pad_add_fusion.info, s32[6,2]{1,0:T(8,128)S(1)} %copy.17.positions, s32[6,256,256]{2,1,0:T(8,128)S(1)} %bitcast.22, f32[2,256,256]{2,1,0:T(8,128)S(1)} %copy-done.4, ...), custom_call_target="tpu_custom_call" | custom-call | flops 805306368 | bytes 8388608 | tf_op jit(solution)/shard_map/pallas_call | solution.py:124
  16.1 4.9 %collective-permute-start.2 = (f32[2,256,128]{2,1,0:T(8,128)S(1)}, f32[2,256,128]{2,1,0:T(8,128)S(1)}, u32[]{:S(2)}, u32[]{:S(2)}) collective-permute-start(f32[2,256,128]{2,1,0:T(8,128)S(1)} %get-tuple-element.48), channel_id=1, source_target_pairs={{1,2},{2,1},{3,4},{4,3},{5,6},{6,5},{7,8},{8,7},{9,10},{10,9},{11,... | collective-permute-start | bytes 786440 | tf_op jit(solution)/shard_map/ppermute | solution.py:450
  22.4 2.9 %collective-permute-start.3 = (f32[2,2,128,128]{3,2,1,0:T(8,128)S(1)}, f32[2,2,128,128]{3,2,1,0:T(8,128)S(1)}, u32[]{:S(2)}, u32[]{:S(2)}) collective-permute-start(f32[2,2,128,128]{3,2,1,0:T(8,128)S(1)} %get-tuple-element.49), channel_id=1, source_target_pairs={{1,2},{2,1},{3,4},{4,3},{5,6},{6,5},{7,8},{8,7},{9,10},{10,9},{11,... | collective-permute-start | bytes 786440 | tf_op jit(solution)/shard_map/ppermute | solution.py:450
  25.3 2.2 %all-gather = f32[4,256,128]{2,1,0:T(8,128)S(1)} all-gather(f32[2,256,128]{2,1,0:T(8,128)S(1)} %get-tuple-element.46), channel_id=2, replica_groups={{0,1},{2,3},{4,5},{6,7},{8,9},{10,11},{12,13},{14,15},{16,17},{18,19},{..., dimensions={0}, use_global_device_ids=true | all-gather | bytes 786432 | tf_op jit(solution)/shard_map/all_gather | solution.py:455
  27.5 2.2 %all-gather.1 = f32[4,2,128,128]{3,2,1,0:T(8,128)S(1)} all-gather(f32[2,2,128,128]{3,2,1,0:T(8,128)S(1)} %get-tuple-element.47), channel_id=3, replica_groups={{0,1},{2,3},{4,5},{6,7},{8,9},{10,11},{12,13},{14,15},{16,17},{18,19},{..., dimensions={0}, use_global_device_ids=true | all-gather | bytes 786432 | tf_op jit(solution)/shard_map/all_gather | solution.py:455
  29.7 2.6 %collective-permute-done.3.refs_3_ = f32[2,2,128,128]{3,2,1,0:T(8,128)S(1)} collective-permute-done((f32[2,2,128,128]{3,2,1,0:T(8,128)S(1)}, f32[2,2,128,128]{3,2,1,0:T(8,128)S(1)}, u32[]{:S(2)}, u32[]{:S(2)}) %collective-permute-start.3) | collective-permute-done | bytes 262176 | tf_op jit(solution)/shard_map/ppermute | solution.py:450
  32.3 3.4 %shard_map.121 = (f32[512,128]{1,0:T(8,128)S(1)}, f32[512,128]{1,0:T(8,128)S(1)}, f32[2,512,128]{2,1,0:T(8,128)S(1)}, f32[2,512,128]{2,1,0:T(8,128)S(1)}, f32[2,512,128]{2,1,0:T(8,128)S(1)}) custom-call(s32[4]{0:T(128)S(1)} %pad_add_fusion.info, s32[6,2]{1,0:T(8,128)S(1)} %copy.17.positions, s32[1,1]{1,0:T(1,128)S(6)} %copy.19.counts, ...), custom_call_target="tpu_custom_call" | custom-call | flops 4831838208 | bytes 8388608 | tf_op jit(solution)/shard_map/pallas_call | solution.py:48
  35.7 7.7 %collective-permute-start.5 = (f32[2,512,128]{2,1,0:T(8,128)S(1)}, f32[2,512,128]{2,1,0:T(8,128)S(1)}, u32[]{:S(2)}, u32[]{:S(2)}) collective-permute-start(f32[2,512,128]{2,1,0:T(8,128)S(1)} %get-tuple-element.58), channel_id=1, source_target_pairs={{1,2},{2,1},{3,4},{4,3},{5,6},{6,5},{7,8},{8,7},{9,10},{10,9},{11,... | collective-permute-start | bytes 1572872 | tf_op jit(solution)/shard_map/ppermute | solution.py:450
  43.4 2.2 %all-gather.2 = f32[1024,128]{1,0:T(8,128)S(1)} all-gather(f32[512,128]{1,0:T(8,128)S(1)} %get-tuple-element.53), channel_id=4, replica_groups={{0,1},{2,3},{4,5},{6,7},{8,9},{10,11},{12,13},{14,15},{16,17},{18,19},{..., dimensions={0}, use_global_device_ids=true | all-gather | bytes 786432 | tf_op jit(solution)/shard_map/all_gather | solution.py:455
  45.6 2.2 %all-gather.3 = f32[1024,128]{1,0:T(8,128)S(1)} all-gather(f32[512,128]{1,0:T(8,128)S(1)} %get-tuple-element.54), channel_id=5, replica_groups={{0,1},{2,3},{4,5},{6,7},{8,9},{10,11},{12,13},{14,15},{16,17},{18,19},{..., dimensions={0}, use_global_device_ids=true | all-gather | bytes 786432 | tf_op jit(solution)/shard_map/all_gather | solution.py:455
  48.4 1.9 %collective-permute-done.5.strip = f32[2,512,128]{2,1,0:T(8,128)S(1)} collective-permute-done((f32[2,512,128]{2,1,0:T(8,128)S(1)}, f32[2,512,128]{2,1,0:T(8,128)S(1)}, u32[]{:S(2)}, u32[]{:S(2)}) %collective-permute-start.5) | collective-permute-done | bytes 524320 | tf_op jit(solution)/shard_map/ppermute | solution.py:450
  50.9 4.1 %collective-permute-start.7 = (f32[2,256,128]{2,1,0:T(8,128)S(1)}, f32[2,256,128]{2,1,0:T(8,128)S(1)}, u32[]{:S(2)}, u32[]{:S(2)}) collective-permute-start(f32[2,256,128]{2,1,0:T(8,128)S(1)} %get-tuple-element.64), channel_id=1, source_target_pairs={{0,16},{16,0},{32,48},{48,32},{64,80},{80,64},{96,112},{112,96},{1... | collective-permute-start | bytes 786440 | tf_op jit(solution)/shard_map/ppermute | solution.py:450
  55.0 4.2 %collective-permute-start.8 = (f32[2,256,128]{2,1,0:T(8,128)S(1)}, f32[2,256,128]{2,1,0:T(8,128)S(1)}, u32[]{:S(2)}, u32[]{:S(2)}) collective-permute-start(f32[2,256,128]{2,1,0:T(8,128)S(1)} %get-tuple-element.65), channel_id=1, source_target_pairs={{16,32},{32,16},{48,64},{64,48},{80,96},{96,80},{17,33},{33,17},{4... | collective-permute-start | bytes 786440 | tf_op jit(solution)/shard_map/ppermute | solution.py:450
  59.2 4.4 %collective-permute-start.4 = (f32[2,256,128]{2,1,0:T(8,128)S(1)}, f32[2,256,128]{2,1,0:T(8,128)S(1)}, u32[]{:S(2)}, u32[]{:S(2)}) collective-permute-start(f32[2,256,128]{2,1,0:T(8,128)S(1)} %get-tuple-element.56), channel_id=1, source_target_pairs={{0,16},{16,0},{32,48},{48,32},{64,80},{80,64},{96,112},{112,96},{1... | collective-permute-start | bytes 786440 | tf_op jit(solution)/shard_map/ppermute | solution.py:450
  63.6 1.9 %collective-permute-start.6 = (f32[2,256,128]{2,1,0:T(8,128)S(1)}, f32[2,256,128]{2,1,0:T(8,128)S(1)}, u32[]{:S(2)}, u32[]{:S(2)}) collective-permute-start(f32[2,256,128]{2,1,0:T(8,128)S(1)} %get-tuple-element.60), channel_id=1, source_target_pairs={{16,32},{32,16},{48,64},{64,48},{80,96},{96,80},{17,33},{33,17},{4... | collective-permute-start | bytes 786440 | tf_op jit(solution)/shard_map/ppermute | solution.py:450
  65.5 4.2 %collective-permute-done.8.halo_b = f32[2,256,128]{2,1,0:T(8,128)S(1)} collective-permute-done((f32[2,256,128]{2,1,0:T(8,128)S(1)}, f32[2,256,128]{2,1,0:T(8,128)S(1)}, u32[]{:S(2)}, u32[]{:S(2)}) %collective-permute-start.8) | collective-permute-done | bytes 262176 | tf_op jit(solution)/shard_map/ppermute | solution.py:450
  70.3 3.0 %collective-permute-start.9 = (f32[2,512,128]{2,1,0:T(8,128)S(1)}, f32[2,512,128]{2,1,0:T(8,128)S(1)}, u32[]{:S(2)}, u32[]{:S(2)}) collective-permute-start(f32[2,512,128]{2,1,0:T(8,128)S(1)} %shard_map.125.ext_b), channel_id=1, source_target_pairs={{1,2},{2,1},{3,4},{4,3},{5,6},{6,5},{7,8},{8,7},{9,10},{10,9},{11,... | collective-permute-start | bytes 1572872 | tf_op jit(solution)/shard_map/ppermute | solution.py:450
  73.4 5.0 %collective-permute-done.6.halo_b = f32[2,256,128]{2,1,0:T(8,128)S(1)} collective-permute-done((f32[2,256,128]{2,1,0:T(8,128)S(1)}, f32[2,256,128]{2,1,0:T(8,128)S(1)}, u32[]{:S(2)}, u32[]{:S(2)}) %collective-permute-start.6) | collective-permute-done | bytes 262176 | tf_op jit(solution)/shard_map/ppermute | solution.py:450
  79.1 2.2 %all-gather.4 = f32[1024,128]{1,0:T(8,128)S(1)} all-gather(f32[512,128]{1,0:T(8,128)S(1)} %get-tuple-element.61.ext_r), channel_id=6, replica_groups={{0,1},{2,3},{4,5},{6,7},{8,9},{10,11},{12,13},{14,15},{16,17},{18,19},{..., dimensions={0}, use_global_device_ids=true | all-gather | bytes 786432 | tf_op jit(solution)/shard_map/all_gather | solution.py:455
  81.3 2.2 %all-gather.5 = f32[1024,128]{1,0:T(8,128)S(1)} all-gather(f32[512,128]{1,0:T(8,128)S(1)} %get-tuple-element.62.ext_i), channel_id=7, replica_groups={{0,1},{2,3},{4,5},{6,7},{8,9},{10,11},{12,13},{14,15},{16,17},{18,19},{..., dimensions={0}, use_global_device_ids=true | all-gather | bytes 786432 | tf_op jit(solution)/shard_map/all_gather | solution.py:455
  83.5 2.4 %collective-permute-done.9.refs_2_ = f32[2,512,128]{2,1,0:T(8,128)S(1)} collective-permute-done((f32[2,512,128]{2,1,0:T(8,128)S(1)}, f32[2,512,128]{2,1,0:T(8,128)S(1)}, u32[]{:S(2)}, u32[]{:S(2)}) %collective-permute-start.9) | collective-permute-done | bytes 524320 | tf_op jit(solution)/shard_map/ppermute | solution.py:450
  85.9 3.4 %shard_map.126 = (f32[2,2,128,128]{3,2,1,0:T(8,128)S(1)}, f32[2,256,128]{2,1,0:T(8,128)S(1)}, f32[2,2,128,128]{3,2,1,0:T(8,128)S(1)}, f32[2,256,128]{2,1,0:T(8,1...) custom-call(s32[4]{0:T(128)S(1)} %pad_add_fusion.info, s32[6,2]{1,0:T(8,128)S(1)} %copy.17.positions, ...), custom_call_target="tpu_custom_call" | custom-call | flops 4831838208 | bytes 8388608 | tf_op jit(solution)/shard_map/pallas_call | solution.py:48
  89.3 6.2 %collective-permute-start.10 = (f32[2,2,128,128]{3,2,1,0:T(8,128)S(1)}, f32[2,2,128,128]{3,2,1,0:T(8,128)S(1)}, u32[]{:S(2)}, u32[]{:S(2)}) collective-permute-start(f32[2,2,128,128]{3,2,1,0:T(8,128)S(1)} %get-tuple-element.69), channel_id=1, source_target_pairs={{1,2},{2,1},{3,4},{4,3},{5,6},{6,5},{7,8},{8,7},{9,10},{10,9},{11,... | collective-permute-start | bytes 786440 | tf_op jit(solution)/shard_map/ppermute | solution.py:450
  95.5 2.2 %all-gather.7 = f32[4,2,128,128]{3,2,1,0:T(8,128)S(1)} all-gather(f32[2,2,128,128]{3,2,1,0:T(8,128)S(1)} %get-tuple-element.70), channel_id=9, replica_groups={{0,1},{2,3},{4,5},{6,7},{8,9},{10,11},{12,13},{14,15},{16,17},{18,19},{..., dimensions={0}, use_global_device_ids=true | all-gather | bytes 786432 | tf_op jit(solution)/shard_map/all_gather | solution.py:455
  100.2 5.8 %collective-permute-start.11 = (f32[2,256,128]{2,1,0:T(8,128)S(1)}, f32[2,256,128]{2,1,0:T(8,128)S(1)}, u32[]{:S(2)}, u32[]{:S(2)}) collective-permute-start(f32[2,256,128]{2,1,0:T(8,128)S(1)} %get-tuple-element.73), channel_id=1, source_target_pairs={{1,2},{2,1},{3,4},{4,3},{5,6},{6,5},{7,8},{8,7},{9,10},{10,9},{11,... | collective-permute-start | bytes 786440 | tf_op jit(solution)/shard_map/ppermute | solution.py:450
  105.9 5.0 %collective-permute-start.13 = (f32[2,128,128]{2,1,0:T(8,128)S(1)}, f32[2,128,128]{2,1,0:T(8,128)S(1)}, u32[]{:S(2)}, u32[]{:S(2)}) collective-permute-start(f32[2,128,128]{2,1,0:T(8,128)S(1)} %get-tuple-element.71.earlier), channel_id=1, source_target_pairs={{16,32},{32,16},{48,64},{64,48},{80,96},{96,80},{17,33},{33,17},{4... | collective-permute-start | bytes 393224 | tf_op jit(solution)/shard_map/ppermute | solution.py:450
  112.1 2.5 %collective-permute-start.14 = (f32[2,128,128]{2,1,0:T(8,128)S(1)}, f32[2,128,128]{2,1,0:T(8,128)S(1)}, u32[]{:S(2)}, u32[]{:S(2)}) collective-permute-start(f32[2,128,128]{2,1,0:T(8,128)S(1)} %get-tuple-element.75), channel_id=1, source_target_pairs={{0,16},{16,0},{32,48},{48,32},{64,80},{80,64},{96,112},{112,96},{1... | collective-permute-start | bytes 393224 | tf_op jit(solution)/shard_map/ppermute | solution.py:450
  114.6 3.2 %collective-permute-start.15 = (f32[2,128,128]{2,1,0:T(8,128)S(1)}, f32[2,128,128]{2,1,0:T(8,128)S(1)}, u32[]{:S(2)}, u32[]{:S(2)}) collective-permute-start(f32[2,128,128]{2,1,0:T(8,128)S(1)} %get-tuple-element.76), channel_id=1, source_target_pairs={{16,32},{32,16},{48,64},{64,48},{80,96},{96,80},{17,33},{33,17},{4... | collective-permute-start | bytes 393224 | tf_op jit(solution)/shard_map/ppermute | solution.py:450
  117.8 2.2 %all-gather.6 = f32[4,256,128]{2,1,0:T(8,128)S(1)} all-gather(f32[2,256,128]{2,1,0:T(8,128)S(1)} %get-tuple-element.68), channel_id=8, replica_groups={{0,1},{2,3},{4,5},{6,7},{8,9},{10,11},{12,13},{14,15},{16,17},{18,19},{..., dimensions={0}, use_global_device_ids=true | all-gather | bytes 786432 | tf_op jit(solution)/shard_map/all_gather | solution.py:455
  121.1 2.7 %collective-permute-done.15.far_b = f32[2,128,128]{2,1,0:T(8,128)S(1)} collective-permute-done((f32[2,128,128]{2,1,0:T(8,128)S(1)}, f32[2,128,128]{2,1,0:T(8,128)S(1)}, u32[]{:S(2)}, u32[]{:S(2)}) %collective-permute-start.15) | collective-permute-done | bytes 131104 | tf_op jit(solution)/shard_map/ppermute | solution.py:450
  (46 shorter events, 16.5 us)
Async XLA Ops:
  0.1 1.0 copy-start
  1.1 20.6 %copy-start.2 = (f32[2,256,256]{2,1,0:T(8,128)S(1)}, f32[2,256,256]{2,1,0:T(8,128)}, u32[]{:S(2)}) copy-start(f32[2,256,256]{2,1,0:T(8,128)} %tile.5) | copy-start | bytes 1572868
  1.7 20.0 %collective-permute-start = (f32[2,128,256]{2,1,0:T(8,128)S(1)}, f32[2,128,256]{2,1,0:T(8,128)S(1)}, u32[]{:S(2)}, u32[]{:S(2)}) collective-permute-start(f32[2,128,256]{2,1,0:T(8,128)S(1)} %get-tuple-element.41), channel_id=1, source_target_pairs={{0,16},{16,0},{32,48},{48,32},{64,80},{80,64},{96,112},{112,96},{1... | collective-permute-start | bytes 786440 | tf_op jit(solution)/shard_map/ppermute | solution.py:450
  3.9 17.8 %collective-permute-start.1 = (f32[2,128,256]{2,1,0:T(8,128)S(1)}, f32[2,128,256]{2,1,0:T(8,128)S(1)}, u32[]{:S(2)}, u32[]{:S(2)}) collective-permute-start(f32[2,128,256]{2,1,0:T(8,128)S(1)} %get-tuple-element.42), channel_id=1, source_target_pairs={{16,32},{32,16},{48,64},{64,48},{80,96},{96,80},{17,33},{33,17},{4... | collective-permute-start | bytes 786440 | tf_op jit(solution)/shard_map/ppermute | solution.py:450
  7.9 1.0 copy-start.1
  8.9 1.4 %copy-start.3 = (s32[1,1,6,256,256]{4,3,2,1,0:T(8,128)S(1)}, s32[1,1,6,256,256]{4,3,2,1,0:T(8,128)}, u32[]{:S(2)}) copy-start(s32[1,1,6,256,256]{4,3,2,1,0:T(8,128)} %param.16) | copy-start | bytes 4718596
  10.3 1.0 copy-start.4
  11.4 0.9 copy-start.10
  16.1 16.2 %copy-start.5 = (bf16[768,256]{1,0:T(8,128)(2,1)S(1)}, bf16[768,256]{1,0:T(8,128)(2,1)}, u32[]{:S(2)}) copy-start(bf16[768,256]{1,0:T(8,128)(2,1)} %constant.46.clone.refs_9_.refs_8_) | copy-start | bytes 1179652
  16.1 16.2 %copy-start.6 = (bf16[256,768]{1,0:T(8,128)(2,1)S(1)}, bf16[256,768]{1,0:T(8,128)(2,1)}, u32[]{:S(2)}) copy-start(bf16[256,768]{1,0:T(8,128)(2,1)} %constant.45.clone.refs_7_.refs_6_) | copy-start | bytes 1179652
  16.1 16.2 %copy-start.7 = (bf16[256,768]{1,0:T(8,128)(2,1)S(1)}, bf16[256,768]{1,0:T(8,128)(2,1)}, u32[]{:S(2)}) copy-start(bf16[256,768]{1,0:T(8,128)(2,1)} %constant.44.clone.refs_8_.refs_7_) | copy-start | bytes 1179652
  16.1 16.1 %copy-start.8 = (bf16[768,256]{1,0:T(8,128)(2,1)S(1)}, bf16[768,256]{1,0:T(8,128)(2,1)}, u32[]{:S(2)}) copy-start(bf16[768,256]{1,0:T(8,128)(2,1)} %constant.43.clone.refs_6_.refs_5_) | copy-start | bytes 1179652
  16.1 16.1 %copy-start.9 = (f32[2,128,256]{2,1,0:T(8,128)S(1)}, f32[2,128,256]{2,1,0:T(8,128)}, u32[]{:S(2)}) copy-start(f32[2,128,256]{2,1,0:T(8,128)} %constant.48.clone.refs_11_.refs_10_) | copy-start | bytes 786436
  16.1 16.1 %copy-start.11 = (f32[2,1,128]{2,1,0:T(1,128)S(1)}, f32[2,1,128]{2,1,0:T(1,128)}, u32[]{:S(2)}) copy-start(f32[2,1,128]{2,1,0:T(1,128)} %constant.47.clone.refs_10_.refs_9_) | copy-start | bytes 3076
  16.1 13.5 %collective-permute-start.2 = (f32[2,256,128]{2,1,0:T(8,128)S(1)}, f32[2,256,128]{2,1,0:T(8,128)S(1)}, u32[]{:S(2)}, u32[]{:S(2)}) collective-permute-start(f32[2,256,128]{2,1,0:T(8,128)S(1)} %get-tuple-element.48), channel_id=1, source_target_pairs={{1,2},{2,1},{3,4},{4,3},{5,6},{6,5},{7,8},{8,7},{9,10},{10,9},{11,... | collective-permute-start | bytes 786440 | tf_op jit(solution)/shard_map/ppermute | solution.py:450
  22.4 9.8 %collective-permute-start.3 = (f32[2,2,128,128]{3,2,1,0:T(8,128)S(1)}, f32[2,2,128,128]{3,2,1,0:T(8,128)S(1)}, u32[]{:S(2)}, u32[]{:S(2)}) collective-permute-start(f32[2,2,128,128]{3,2,1,0:T(8,128)S(1)} %get-tuple-element.49), channel_id=1, source_target_pairs={{1,2},{2,1},{3,4},{4,3},{5,6},{6,5},{7,8},{8,7},{9,10},{10,9},{11,... | collective-permute-start | bytes 786440 | tf_op jit(solution)/shard_map/ppermute | solution.py:450
  35.7 14.5 %collective-permute-start.5 = (f32[2,512,128]{2,1,0:T(8,128)S(1)}, f32[2,512,128]{2,1,0:T(8,128)S(1)}, u32[]{:S(2)}, u32[]{:S(2)}) collective-permute-start(f32[2,512,128]{2,1,0:T(8,128)S(1)} %get-tuple-element.58), channel_id=1, source_target_pairs={{1,2},{2,1},{3,4},{4,3},{5,6},{6,5},{7,8},{8,7},{9,10},{10,9},{11,... | collective-permute-start | bytes 1572872 | tf_op jit(solution)/shard_map/ppermute | solution.py:450
  50.9 14.6 %collective-permute-start.7 = (f32[2,256,128]{2,1,0:T(8,128)S(1)}, f32[2,256,128]{2,1,0:T(8,128)S(1)}, u32[]{:S(2)}, u32[]{:S(2)}) collective-permute-start(f32[2,256,128]{2,1,0:T(8,128)S(1)} %get-tuple-element.64), channel_id=1, source_target_pairs={{0,16},{16,0},{32,48},{48,32},{64,80},{80,64},{96,112},{112,96},{1... | collective-permute-start | bytes 786440 | tf_op jit(solution)/shard_map/ppermute | solution.py:450
  55.0 14.7 %collective-permute-start.8 = (f32[2,256,128]{2,1,0:T(8,128)S(1)}, f32[2,256,128]{2,1,0:T(8,128)S(1)}, u32[]{:S(2)}, u32[]{:S(2)}) collective-permute-start(f32[2,256,128]{2,1,0:T(8,128)S(1)} %get-tuple-element.65), channel_id=1, source_target_pairs={{16,32},{32,16},{48,64},{64,48},{80,96},{96,80},{17,33},{33,17},{4... | collective-permute-start | bytes 786440 | tf_op jit(solution)/shard_map/ppermute | solution.py:450
  59.2 14.3 %collective-permute-start.4 = (f32[2,256,128]{2,1,0:T(8,128)S(1)}, f32[2,256,128]{2,1,0:T(8,128)S(1)}, u32[]{:S(2)}, u32[]{:S(2)}) collective-permute-start(f32[2,256,128]{2,1,0:T(8,128)S(1)} %get-tuple-element.56), channel_id=1, source_target_pairs={{0,16},{16,0},{32,48},{48,32},{64,80},{80,64},{96,112},{112,96},{1... | collective-permute-start | bytes 786440 | tf_op jit(solution)/shard_map/ppermute | solution.py:450
  63.6 14.9 %collective-permute-start.6 = (f32[2,256,128]{2,1,0:T(8,128)S(1)}, f32[2,256,128]{2,1,0:T(8,128)S(1)}, u32[]{:S(2)}, u32[]{:S(2)}) collective-permute-start(f32[2,256,128]{2,1,0:T(8,128)S(1)} %get-tuple-element.60), channel_id=1, source_target_pairs={{16,32},{32,16},{48,64},{64,48},{80,96},{96,80},{17,33},{33,17},{4... | collective-permute-start | bytes 786440 | tf_op jit(solution)/shard_map/ppermute | solution.py:450
  70.3 15.5 %collective-permute-start.9 = (f32[2,512,128]{2,1,0:T(8,128)S(1)}, f32[2,512,128]{2,1,0:T(8,128)S(1)}, u32[]{:S(2)}, u32[]{:S(2)}) collective-permute-start(f32[2,512,128]{2,1,0:T(8,128)S(1)} %shard_map.125.ext_b), channel_id=1, source_target_pairs={{1,2},{2,1},{3,4},{4,3},{5,6},{6,5},{7,8},{8,7},{9,10},{10,9},{11,... | collective-permute-start | bytes 1572872 | tf_op jit(solution)/shard_map/ppermute | solution.py:450
  89.3 10.3 %collective-permute-start.10 = (f32[2,2,128,128]{3,2,1,0:T(8,128)S(1)}, f32[2,2,128,128]{3,2,1,0:T(8,128)S(1)}, u32[]{:S(2)}, u32[]{:S(2)}) collective-permute-start(f32[2,2,128,128]{3,2,1,0:T(8,128)S(1)} %get-tuple-element.69), channel_id=1, source_target_pairs={{1,2},{2,1},{3,4},{4,3},{5,6},{6,5},{7,8},{8,7},{9,10},{10,9},{11,... | collective-permute-start | bytes 786440 | tf_op jit(solution)/shard_map/ppermute | solution.py:450
  100.2 23.7 %collective-permute-start.11 = (f32[2,256,128]{2,1,0:T(8,128)S(1)}, f32[2,256,128]{2,1,0:T(8,128)S(1)}, u32[]{:S(2)}, u32[]{:S(2)}) collective-permute-start(f32[2,256,128]{2,1,0:T(8,128)S(1)} %get-tuple-element.73), channel_id=1, source_target_pairs={{1,2},{2,1},{3,4},{4,3},{5,6},{6,5},{7,8},{8,7},{9,10},{10,9},{11,... | collective-permute-start | bytes 786440 | tf_op jit(solution)/shard_map/ppermute | solution.py:450
  105.9 14.0 %collective-permute-start.13 = (f32[2,128,128]{2,1,0:T(8,128)S(1)}, f32[2,128,128]{2,1,0:T(8,128)S(1)}, u32[]{:S(2)}, u32[]{:S(2)}) collective-permute-start(f32[2,128,128]{2,1,0:T(8,128)S(1)} %get-tuple-element.71.earlier), channel_id=1, source_target_pairs={{16,32},{32,16},{48,64},{64,48},{80,96},{96,80},{17,33},{33,17},{4... | collective-permute-start | bytes 393224 | tf_op jit(solution)/shard_map/ppermute | solution.py:450
  111.0 9.0 %collective-permute-start.12 = (f32[2,128,128]{2,1,0:T(8,128)S(1)}, f32[2,128,128]{2,1,0:T(8,128)S(1)}, u32[]{:S(2)}, u32[]{:S(2)}) collective-permute-start(f32[2,128,128]{2,1,0:T(8,128)S(1)} %get-tuple-element.74), channel_id=1, source_target_pairs={{0,16},{16,0},{32,48},{48,32},{64,80},{80,64},{96,112},{112,96},{1... | collective-permute-start | bytes 393224 | tf_op jit(solution)/shard_map/ppermute | solution.py:450
  112.1 9.1 %collective-permute-start.14 = (f32[2,128,128]{2,1,0:T(8,128)S(1)}, f32[2,128,128]{2,1,0:T(8,128)S(1)}, u32[]{:S(2)}, u32[]{:S(2)}) collective-permute-start(f32[2,128,128]{2,1,0:T(8,128)S(1)} %get-tuple-element.75), channel_id=1, source_target_pairs={{0,16},{16,0},{32,48},{48,32},{64,80},{80,64},{96,112},{112,96},{1... | collective-permute-start | bytes 393224 | tf_op jit(solution)/shard_map/ppermute | solution.py:450
  114.6 9.3 %collective-permute-start.15 = (f32[2,128,128]{2,1,0:T(8,128)S(1)}, f32[2,128,128]{2,1,0:T(8,128)S(1)}, u32[]{:S(2)}, u32[]{:S(2)}) collective-permute-start(f32[2,128,128]{2,1,0:T(8,128)S(1)} %get-tuple-element.76), channel_id=1, source_target_pairs={{16,32},{32,16},{48,64},{64,48},{80,96},{96,80},{17,33},{33,17},{4... | collective-permute-start | bytes 393224 | tf_op jit(solution)/shard_map/ppermute | solution.py:450
where the time goes:
time: 125 us
  starting transfers between devices  62.3 us (50%)
  waiting for transfers between devices  21.2 us (17%)
  blocking collectives  17.4 us (14%)
  Pallas kernels  17.1 us (14%)
  local copies, waits for them, and re-layouts  6.25 us (5%)
    ppermute x16, starting transfers between devices, swapped(): return lax.ppermute(value, axis, route)  62.3 us
    ppermute x16, waiting for transfers between devices, swapped(): return lax.ppermute(value, axis, route)  21.2 us
    all_gather x8, blocking collectives, paired(): return lax.all_gather(value, 'cols', axis_index_groups=groups)  17.4 us
    pallas_call x11, Pallas kernels, whole(): pl.pallas_call(body, out_shape=outs, in_specs=[SMEM] * len(scalars) + [VM...  13.4 us
    unnamed x24, local copies, waits for them, and re-layouts  5.48 us
    pallas_call x1, Pallas kernels, prepare(): pl.pallas_call(prepare_body, out_shape=(shaped(slots, 2, half, size), sha...  3.78 us
  transfers between devices with their start and end apart: 16, of which 9 were waited for; matrix products, arithmetic and copies ran while one was open for 1% of the time, Pallas kernels for 6%

commit v1 on v0

--- a/solution.py
+++ b/solution.py
@@ -71,15 +71,14 @@
         side_b[...] = tile[:, :, left]
 
 
-def cut_rows_body(info, tile, edge_a, edge_b):
+def cut_body(info, tile, edge_a, edge_b, side_a, side_b):
     edge = tile.shape[1] - MARGIN
     edge_a[...] = tile[:, pl.ds(pl.multiple_of((1 - info[0]) * edge, 8), MARGIN), :]
     edge_b[...] = tile[:, pl.ds(pl.multiple_of(info[0] * edge, 8), MARGIN), :]
-
-
-def prepare_body(
-    info, positions, intensity, probe, order, tile, measured, rolled, edge_a, edge_b, held, arrived
-):
+    split_columns(info[1], tile, side_a, side_b)
+
+
+def prepare_body(positions, intensity, probe, order, measured, rolled, held, arrived):
     slots, size = intensity.shape[0], probe.shape[1]
     half = size // 2
     moves = [order[:half], order[half:]]
@@ -89,7 +88,6 @@
     ]
     for copy in copies:
         copy.start()
-    split_columns(info[1], tile, edge_a, edge_b)
 
     def turn(slot, carry):
         shift = lax.rem(positions[slot, 1], size)
@@ -117,19 +115,18 @@
     lax.fori_loop(0, slots, reorder, 0)
 
 
-def prepare(info, positions, intensity, probe, order, tile):
+def prepare(positions, intensity, probe, order):
     slots, size = intensity.shape[0], probe.shape[1]
-    edge = shaped(2, tile.shape[1], MARGIN)
     half = size // 2
     return pl.pallas_call(
         prepare_body,
-        out_shape=(shaped(slots, 2, half, size), shaped(slots, 2, size, size), edge, edge),
-        in_specs=[SMEM, SMEM, pl.BlockSpec(memory_space=pl.ANY), VMEM, VMEM, VMEM],
-        out_specs=(VMEM,) * 4,
+        out_shape=(shaped(slots, 2, half, size), shaped(slots, 2, size, size)),
+        in_specs=[SMEM, pl.BlockSpec(memory_space=pl.ANY), VMEM, VMEM],
+        out_specs=(VMEM, VMEM),
         scratch_shapes=[pltpu.VMEM((2, slots, size, half), jnp.int32), pltpu.SemaphoreType.DMA((2,))],
         compiler_params=pltpu.CompilerParams(vmem_limit_bytes=24 << 20),
         cost_estimate=pl.CostEstimate(flops=slots * 2**27, bytes_accessed=8 << 20, transcendentals=0),
-    )(info, positions, intensity, probe, order, tile)
+    )(positions, intensity, probe, order)
 
 
 def halves(value):
@@ -342,39 +339,23 @@
         fill(right, left)
 
 
-def outgoing(odd_row, total, width, out_a, out_b):
-    extent = total.shape[1]
-    out_a[...] = total[:, pl.ds(pl.multiple_of((1 - odd_row) * (extent - width), 8), width), :]
-    out_b[...] = total[:, pl.ds(pl.multiple_of(odd_row * (extent - width), 8), width), :]
-
-
-def join_near_body(info, inner, near_r, near_i, total, out_a, out_b):
+def join_body(info, inner_a, inner_b, near_r, near_i, far, total, out_a, out_b):
     other = 1 - info[1]
-    total[0] = inner[0] + near_r[other]
-    total[1] = inner[1] + near_i[other]
-    outgoing(info[0], total, total.shape[1] // 2, out_a, out_b)
-
-
-def join_far_body(info, inner, strip, waiting, total, out_a, out_b, passed):
-    total[...] = inner[...] + strip[...]
-    outgoing(info[0], total, total.shape[1] // 2, out_a, out_b)
-    passed[...] = waiting[...]
-
-
-def corner_near_body(info, inner, corner, out_a, out_b):
-    add_corner(info, inner, corner.at[1 - info[1]], out_a, out_b)
-
-
-def corner_far_body(info, inner, corner, earlier, waiting, out_a, out_b, passed):
-    add_corner(info, inner, corner, out_a, out_b)
-    passed[...] = waiting[...]
-
-
-def add_corner(info, inner, corner, out_a, out_b):
-    last = inner.shape[1] - MARGIN
-    lower, upper = 1 - info[0], info[0]
-    out_a[...] = inner[:, pl.ds(pl.multiple_of(lower * last, 8), MARGIN), :] + corner[lower]
-    out_b[...] = inner[:, pl.ds(pl.multiple_of(upper * last, 8), MARGIN), :] + corner[upper]
+    total[0, 0] = inner_a[0] + near_r[other]
+    total[0, 1] = inner_a[1] + near_i[other]
+    total[1] = inner_b[...] + far[...]
+    middle = total.shape[2] // 2
+    out_a[...] = total[:, :, pl.ds(pl.multiple_of((1 - info[0]) * middle, 8), middle), :]
+    out_b[...] = total[:, :, pl.ds(pl.multiple_of(info[0] * middle, 8), middle), :]
+
+
+def corner_body(info, inner_a, inner_b, near, far, edge, out_a, out_b, passed):
+    last = inner_a.shape[1] - MARGIN
+    for out, side in ((out_a, 1 - info[0]), (out_b, info[0])):
+        rows = pl.ds(pl.multiple_of(side * last, 8), MARGIN)
+        out[0] = inner_a[:, rows, :] + near[1 - info[1], side]
+        out[1] = inner_b[:, rows, :] + far[side]
+    passed[...] = edge[...]
 
 
 def updated(info, part, ext, total, halo_a, halo_b):
@@ -387,18 +368,15 @@
     return tall(ext[:middle] - step_rate * above, ext[middle:] - step_rate * below)
 
 
-def update_near_body(info, ext_r, ext_i, total, halo_a, halo_b, out_r, out_i):
-    out_r[...] = updated(info, 0, ext_r, total, halo_a, halo_b)
-    out_i[...] = updated(info, 1, ext_i, total, halo_a, halo_b)
-
-
-def update_far_body(info, ext_b, total, halo_a, halo_b, out):
+def update_body(info, ext_r, ext_i, ext_b, total, halo_a, halo_b, out_r, out_i, out_b):
+    out_r[...] = updated(info, 0, ext_r, total.at[0], halo_a.at[0], halo_b.at[0])
+    out_i[...] = updated(info, 1, ext_i, total.at[0], halo_a.at[0], halo_b.at[0])
     for part in range(2):
-        out[part] = updated(info, part, ext_b.at[part], total, halo_a, halo_b)
+        out_b[part] = updated(info, part, ext_b.at[part], total.at[1], halo_a.at[1], halo_b.at[1])
 
 
 def finish_body(
-    info, ext_r, ext_i, ext_b, inner_a, inner_b, edge_a, edge_b, near_a, near_b, far_a, far_b, out
+    info, ext_r, ext_i, ext_b, inner_a, inner_b, edge_a, edge_b, halo_a, halo_b, out
 ):
     size = out.shape[1]
     half = size // 2
@@ -414,8 +392,8 @@
             out[part, half:, cut] = ext[part][lower] - step_rate * below
 
     def place(cut_a, cut_b):
-        settle(cut_a, [ext_r, ext_i], inner_a, edge_a.at[1 - info[1]], near_a, near_b)
-        settle(cut_b, [ext_b.at[0], ext_b.at[1]], inner_b, edge_b, far_a, far_b)
+        settle(cut_a, [ext_r, ext_i], inner_a, edge_a.at[1 - info[1]], halo_a.at[0], halo_b.at[0])
+        settle(cut_b, [ext_b.at[0], ext_b.at[1]], inner_b, edge_b, halo_a.at[1], halo_b.at[1])
 
     left, right = slice(0, HALF), slice(HALF, 2 * HALF)
 
@@ -472,10 +450,11 @@
     plane, strip = shaped(extent, HALF), shaped(2, extent, HALF)
     corner = shaped(2, 2, MARGIN, HALF)
 
-    edge = shaped(2, MARGIN, tile)
-    halos = both_rows(*whole(cut_rows_body, (edge, edge), (info,), (object_field,)))
-    measured, rolled, edge_a, edge_b = prepare(info, positions, intensity, probe, order, object_field)
-    far_edge, near_edge = swapped(edge_b, "cols", 1), paired(edge_a)
+    edge, side = shaped(2, MARGIN, tile), shaped(2, tile, MARGIN)
+    edge_a, edge_b, side_a, side_b = whole(cut_body, (edge, edge, side, side), (info,), (object_field,))
+    halos = both_rows(edge_a, edge_b)
+    far_edge, near_edge = swapped(side_b, "cols", 1), paired(side_a)
+    measured, rolled = prepare(positions, intensity, probe, order)
     *ext, corner_a, corner_b = whole(
         extend_body, (plane, plane, strip, corner, corner), (info,), (object_field, *halos)
     )
@@ -487,36 +466,25 @@
 
     far = swapped(out_b, "cols", 1)
     near = paired(out_r), paired(out_i)
-    piece = shaped(2, extent // 2, HALF)
-    total_a, edge_a, edge_b = whole(join_near_body, (strip, piece, piece), (info,), (in_a, *near))
-    near_halo_a = swapped(edge_a, "rows", 0)
-    total_b, far_a, far_b, edge_b = whole(
-        join_far_body, (strip, piece, piece, piece), (info,), (in_b, far, edge_b)
-    )
-    far_halos = both_rows(far_a, far_b)
-    near_halos = near_halo_a, swapped(edge_b, "rows", 1)
-    far_ext = whole(update_far_body, (strip,), (info,), (ext[2], total_b, *far_halos))
-    near_ext = whole(update_near_body, (plane, plane), (info,), (*ext[:2], total_a, *near_halos))
-    ext = (*near_ext, *far_ext)
+    piece = shaped(2, 2, extent // 2, HALF)
+    total, edge_a, edge_b = whole(
+        join_body, (shaped(2, 2, extent, HALF), piece, piece), (info,), (in_a, in_b, *near, far)
+    )
+    halos = both_rows(edge_a, edge_b)
+    ext = whole(update_body, (plane, plane, strip), (info,), (*ext, total, *halos))
     sides = paired(ext[0]), paired(ext[1]), swapped(ext[2], "cols", 1)
     corner_a, edge_a, corner_b, edge_b, in_a, in_b = gradient(
         False, info, positions, counts, ext, sides, measured, rolled, tables
     )
 
-    piece = shaped(2, MARGIN, HALF)
+    piece = shaped(2, 2, MARGIN, HALF)
     far_corner = swapped(corner_b, "cols", 1)
-    near_corner = paired(corner_a)
-    rows_a, rows_b = whole(corner_near_body, (piece, piece), (info,), (in_a, near_corner))
-    near_halos = both_rows(rows_a, rows_b)
-    edge = shaped(2, tile, HALF)
-    far_a, far_b, edge_b = whole(
-        corner_far_body, (piece, piece, edge), (info,), (in_b, far_corner, rows_b, edge_b)
-    )
-    far_halos = both_rows(far_a, far_b)
+    rows_a, rows_b, edge_b = whole(
+        corner_body, (piece, piece, side), (info,), (in_a, in_b, paired(corner_a), far_corner, edge_b)
+    )
+    halos = both_rows(rows_a, rows_b)
     sides = paired(edge_a), swapped(edge_b, "cols", 1)
-    return whole(
-        finish_body, (shaped(2, tile, tile),), (info,), (*ext, in_a, in_b, *sides, *near_halos, *far_halos)
-    )[0]
+    return whole(finish_body, (shaped(2, tile, tile),), (info,), (*ext, in_a, in_b, *sides, *halos))[0]
 
 
 def solution(mesh):

time: 125 us -> 127 us (1.016); the launches traced: 125 us -> 125 us
  starting transfers between devices: 62.3 us -> 38.4 us
  waiting for transfers between devices: 21.2 us -> 38.1 us
  Pallas kernels: 17.1 us -> 25 us
    ppermute x16 -> x12, starting transfers between devices: 62.3 us -> 38.4 us  [swapped(): return lax.ppermute(value, axis, route)]
    ppermute x16 -> x12, waiting for transfers between devices: 21.2 us -> 38.1 us  [swapped(): return lax.ppermute(value, axis, route)]
    pallas_call x11 -> x8, Pallas kernels: 13.4 us -> 21.3 us  [whole(): pl.pallas_call(body, out_shape=outs, in_specs=[SMEM] * len(scalars) + [VM...]
    unnamed x24 -> x22, local copies, waits for them, and re-layouts: 5.48 us -> 4.44 us
  transfers between devices with their start and end apart: 16 -> 12, of which waited for: 9 -> 9; matrix products, arithmetic and copies ran while one was open for 1% -> 1% of each run, Pallas kernels for 6% -> 4%
where the time goes in v1:
time: 127 us; the launch traced here: 125 us
  starting transfers between devices  38.4 us (30%)
  waiting for transfers between devices  38.1 us (30%)
  Pallas kernels  25 us (20%)
  blocking collectives  17.4 us (14%)
  local copies, waits for them, and re-layouts  5.21 us (4%)
    ppermute x12, starting transfers between devices, swapped(): return lax.ppermute(value, axis, route)  38.4 us
    ppermute x12, waiting for transfers between devices, swapped(): return lax.ppermute(value, axis, route)  38.1 us
    pallas_call x8, Pallas kernels, whole(): pl.pallas_call(body, out_shape=outs, in_specs=[SMEM] * len(scalars) + [VM...  21.3 us
    all_gather x8, blocking collectives, paired(): return lax.all_gather(value, 'cols', axis_index_groups=groups)  17.4 us
    unnamed x22, local copies, waits for them, and re-layouts  4.44 us
    pallas_call x1, Pallas kernels, prepare(): pl.pallas_call(prepare_body, out_shape=(shaped(slots, 2, half, size), sha...  3.73 us
  transfers between devices with their start and end apart: 12, of which 9 were waited for; matrix products, arithmetic and copies ran while one was open for 1% of the time, Pallas kernels for 4%

profile of v1, /device:TPU:10, one launch (start us, length us, event | category | flops | bytes accessed | tf_op | source)
XLA Modules:
  0.0 125.1 jit_solution(16615461186034092265)
XLA Ops:
  1.8 2.2 %collective-permute-start = (f32[2,128,256]{2,1,0:T(8,128)S(1)}, f32[2,128,256]{2,1,0:T(8,128)S(1)}, u32[]{:S(2)}, u32[]{:S(2)}) collective-permute-start(f32[2,128,256]{2,1,0:T(8,128)S(1)} %get-tuple-element.36), channel_id=1, source_target_pairs={{0,16},{16,0},{32,48},{48,32},{64,80},{80,64},{96,112},{112,96},{1... | collective-permute-start | bytes 786440 | tf_op jit(solution)/shard_map/ppermute | solution.py:428
  4.0 3.2 %collective-permute-start.1 = (f32[2,128,256]{2,1,0:T(8,128)S(1)}, f32[2,128,256]{2,1,0:T(8,128)S(1)}, u32[]{:S(2)}, u32[]{:S(2)}) collective-permute-start(f32[2,128,256]{2,1,0:T(8,128)S(1)} %get-tuple-element.37), channel_id=1, source_target_pairs={{16,32},{32,16},{48,64},{64,48},{80,96},{96,80},{17,33},{33,17},{4... | collective-permute-start | bytes 786440 | tf_op jit(solution)/shard_map/ppermute | solution.py:428
  7.2 4.8 %collective-permute-start.2 = (f32[2,256,128]{2,1,0:T(8,128)S(1)}, f32[2,256,128]{2,1,0:T(8,128)S(1)}, u32[]{:S(2)}, u32[]{:S(2)}) collective-permute-start(f32[2,256,128]{2,1,0:T(8,128)S(1)} %get-tuple-element.43), channel_id=1, source_target_pairs={{1,2},{2,1},{3,4},{4,3},{5,6},{6,5},{7,8},{8,7},{9,10},{10,9},{11,... | collective-permute-start | bytes 786440 | tf_op jit(solution)/shard_map/ppermute | solution.py:428
  16.7 3.7 %shard_map.120 = (f32[6,2,128,256]{3,2,1,0:T(8,128)S(1)}, f32[6,2,256,256]{3,2,1,0:T(8,128)S(1)}) custom-call(s32[6,2]{1,0:T(8,128)S(1)} %copy.17.positions, s32[6,256,256]{2,1,0:T(8,128)S(1)} %bitcast.22, f32[2,256,256]{2,1,0:T(8,128)S(1)} %copy-done.3, bf16[256,256]{1,0:T(8,128)(2,1)S(1)} %copy-done.9), custom_call_target="tpu_custom_call" | custom-call | flops 805306368 | bytes 8388608 | tf_op jit(solution)/shard_map/pallas_call | solution.py:121
  21.3 2.9 %collective-permute-start.3 = (f32[2,2,128,128]{3,2,1,0:T(8,128)S(1)}, f32[2,2,128,128]{3,2,1,0:T(8,128)S(1)}, u32[]{:S(2)}, u32[]{:S(2)}) collective-permute-start(f32[2,2,128,128]{3,2,1,0:T(8,128)S(1)} %get-tuple-element.44), channel_id=1, source_target_pairs={{1,2},{2,1},{3,4},{4,3},{5,6},{6,5},{7,8},{8,7},{9,10},{10,9},{11,... | collective-permute-start | bytes 786440 | tf_op jit(solution)/shard_map/ppermute | solution.py:428
  24.1 2.2 %all-gather = f32[4,256,128]{2,1,0:T(8,128)S(1)} all-gather(f32[2,256,128]{2,1,0:T(8,128)S(1)} %get-tuple-element.41), channel_id=2, replica_groups={{0,1},{2,3},{4,5},{6,7},{8,9},{10,11},{12,13},{14,15},{16,17},{18,19},{..., dimensions={0}, use_global_device_ids=true | all-gather | bytes 786432 | tf_op jit(solution)/shard_map/all_gather | solution.py:433
  26.3 2.2 %all-gather.1 = f32[4,2,128,128]{3,2,1,0:T(8,128)S(1)} all-gather(f32[2,2,128,128]{3,2,1,0:T(8,128)S(1)} %get-tuple-element.42), channel_id=3, replica_groups={{0,1},{2,3},{4,5},{6,7},{8,9},{10,11},{12,13},{14,15},{16,17},{18,19},{..., dimensions={0}, use_global_device_ids=true | all-gather | bytes 786432 | tf_op jit(solution)/shard_map/all_gather | solution.py:433
  28.5 2.6 %collective-permute-done.3.refs_3_ = f32[2,2,128,128]{3,2,1,0:T(8,128)S(1)} collective-permute-done((f32[2,2,128,128]{3,2,1,0:T(8,128)S(1)}, f32[2,2,128,128]{3,2,1,0:T(8,128)S(1)}, u32[]{:S(2)}, u32[]{:S(2)}) %collective-permute-start.3) | collective-permute-done | bytes 262176 | tf_op jit(solution)/shard_map/ppermute | solution.py:428
  31.1 8.2 %shard_map.121 = (f32[512,128]{1,0:T(8,128)S(1)}, f32[512,128]{1,0:T(8,128)S(1)}, f32[2,512,128]{2,1,0:T(8,128)S(1)}, f32[2,512,128]{2,1,0:T(8,128)S(1)}, f32[2,512,128]{2,1,0:T(8,128)S(1)}) custom-call(s32[4]{0:T(128)S(1)} %pad_add_fusion.info, s32[6,2]{1,0:T(8,128)S(1)} %copy.17.positions, s32[1,1]{1,0:T(1,128)S(6)} %copy.19.counts, ...), custom_call_target="tpu_custom_call" | custom-call | flops 4831838208 | bytes 8388608 | tf_op jit(solution)/shard_map/pallas_call | solution.py:48
  39.3 1.9 %collective-permute-start.4 = (f32[2,512,128]{2,1,0:T(8,128)S(1)}, f32[2,512,128]{2,1,0:T(8,128)S(1)}, u32[]{:S(2)}, u32[]{:S(2)}) collective-permute-start(f32[2,512,128]{2,1,0:T(8,128)S(1)} %get-tuple-element.51), channel_id=1, source_target_pairs={{1,2},{2,1},{3,4},{4,3},{5,6},{6,5},{7,8},{8,7},{9,10},{10,9},{11,... | collective-permute-start | bytes 1572872 | tf_op jit(solution)/shard_map/ppermute | solution.py:428
  41.3 2.2 %all-gather.2 = f32[1024,128]{1,0:T(8,128)S(1)} all-gather(f32[512,128]{1,0:T(8,128)S(1)} %get-tuple-element.49), channel_id=4, replica_groups={{0,1},{2,3},{4,5},{6,7},{8,9},{10,11},{12,13},{14,15},{16,17},{18,19},{..., dimensions={0}, use_global_device_ids=true | all-gather | bytes 786432 | tf_op jit(solution)/shard_map/all_gather | solution.py:433
  43.4 2.2 %all-gather.3 = f32[1024,128]{1,0:T(8,128)S(1)} all-gather(f32[512,128]{1,0:T(8,128)S(1)} %get-tuple-element.50), channel_id=5, replica_groups={{0,1},{2,3},{4,5},{6,7},{8,9},{10,11},{12,13},{14,15},{16,17},{18,19},{..., dimensions={0}, use_global_device_ids=true | all-gather | bytes 786432 | tf_op jit(solution)/shard_map/all_gather | solution.py:433
  45.6 6.3 %collective-permute-done.4.far = f32[2,512,128]{2,1,0:T(8,128)S(1)} collective-permute-done((f32[2,512,128]{2,1,0:T(8,128)S(1)}, f32[2,512,128]{2,1,0:T(8,128)S(1)}, u32[]{:S(2)}, u32[]{:S(2)}) %collective-permute-start.4) | collective-permute-done | bytes 524320 | tf_op jit(solution)/shard_map/ppermute | solution.py:428
  52.7 3.7 %collective-permute-start.5 = (f32[2,2,256,128]{3,2,1,0:T(8,128)S(1)}, f32[2,2,256,128]{3,2,1,0:T(8,128)S(1)}, u32[]{:S(2)}, u32[]{:S(2)}) collective-permute-start(f32[2,2,256,128]{3,2,1,0:T(8,128)S(1)} %get-tuple-element.53), channel_id=1, source_target_pairs={{0,16},{16,0},{32,48},{48,32},{64,80},{80,64},{96,112},{112,96},{1... | collective-permute-start | bytes 1572872 | tf_op jit(solution)/shard_map/ppermute | solution.py:428
  56.3 1.9 %collective-permute-start.6 = (f32[2,2,256,128]{3,2,1,0:T(8,128)S(1)}, f32[2,2,256,128]{3,2,1,0:T(8,128)S(1)}, u32[]{:S(2)}, u32[]{:S(2)}) collective-permute-start(f32[2,2,256,128]{3,2,1,0:T(8,128)S(1)} %get-tuple-element.54), channel_id=1, source_target_pairs={{16,32},{32,16},{48,64},{64,48},{80,96},{96,80},{17,33},{33,17},{4... | collective-permute-start | bytes 1572872 | tf_op jit(solution)/shard_map/ppermute | solution.py:428
  58.3 10.7 %collective-permute-done.5.halo_a = f32[2,2,256,128]{3,2,1,0:T(8,128)S(1)} collective-permute-done((f32[2,2,256,128]{3,2,1,0:T(8,128)S(1)}, f32[2,2,256,128]{3,2,1,0:T(8,128)S(1)}, u32[]{:S(2)}, u32[]{:S(2)}) %collective-permute-start.5) | collective-permute-done | bytes 524320 | tf_op jit(solution)/shard_map/ppermute | solution.py:428
  68.9 3.8 %collective-permute-done.6.halo_b = f32[2,2,256,128]{3,2,1,0:T(8,128)S(1)} collective-permute-done((f32[2,2,256,128]{3,2,1,0:T(8,128)S(1)}, f32[2,2,256,128]{3,2,1,0:T(8,128)S(1)}, u32[]{:S(2)}, u32[]{:S(2)}) %collective-permute-start.6) | collective-permute-done | bytes 524320 | tf_op jit(solution)/shard_map/ppermute | solution.py:428
  73.5 6.9 %collective-permute-start.7 = (f32[2,512,128]{2,1,0:T(8,128)S(1)}, f32[2,512,128]{2,1,0:T(8,128)S(1)}, u32[]{:S(2)}, u32[]{:S(2)}) collective-permute-start(f32[2,512,128]{2,1,0:T(8,128)S(1)} %get-tuple-element.57.ext_b), channel_id=1, source_target_pairs={{1,2},{2,1},{3,4},{4,3},{5,6},{6,5},{7,8},{8,7},{9,10},{10,9},{11,... | collective-permute-start | bytes 1572872 | tf_op jit(solution)/shard_map/ppermute | solution.py:428
  80.4 2.2 %all-gather.4 = f32[1024,128]{1,0:T(8,128)S(1)} all-gather(f32[512,128]{1,0:T(8,128)S(1)} %get-tuple-element.55.ext_r), channel_id=6, replica_groups={{0,1},{2,3},{4,5},{6,7},{8,9},{10,11},{12,13},{14,15},{16,17},{18,19},{..., dimensions={0}, use_global_device_ids=true | all-gather | bytes 786432 | tf_op jit(solution)/shard_map/all_gather | solution.py:433
  82.6 2.2 %all-gather.5 = f32[1024,128]{1,0:T(8,128)S(1)} all-gather(f32[512,128]{1,0:T(8,128)S(1)} %get-tuple-element.56.ext_i), channel_id=7, replica_groups={{0,1},{2,3},{4,5},{6,7},{8,9},{10,11},{12,13},{14,15},{16,17},{18,19},{..., dimensions={0}, use_global_device_ids=true | all-gather | bytes 786432 | tf_op jit(solution)/shard_map/all_gather | solution.py:433
  84.8 2.5 %collective-permute-done.7.refs_2_ = f32[2,512,128]{2,1,0:T(8,128)S(1)} collective-permute-done((f32[2,512,128]{2,1,0:T(8,128)S(1)}, f32[2,512,128]{2,1,0:T(8,128)S(1)}, u32[]{:S(2)}, u32[]{:S(2)}) %collective-permute-start.7) | collective-permute-done | bytes 524320 | tf_op jit(solution)/shard_map/ppermute | solution.py:428
  87.3 8.2 %shard_map.124 = (f32[2,2,128,128]{3,2,1,0:T(8,128)S(1)}, f32[2,256,128]{2,1,0:T(8,128)S(1)}, f32[2,2,128,128]{3,2,1,0:T(8,128)S(1)}, f32[2,256,128]{2,1,0:T(8,1...) custom-call(s32[4]{0:T(128)S(1)} %pad_add_fusion.info, s32[6,2]{1,0:T(8,128)S(1)} %copy.17.positions, ...), custom_call_target="tpu_custom_call" | custom-call | flops 4831838208 | bytes 8388608 | tf_op jit(solution)/shard_map/pallas_call | solution.py:48
  95.5 1.9 %collective-permute-start.8 = (f32[2,2,128,128]{3,2,1,0:T(8,128)S(1)}, f32[2,2,128,128]{3,2,1,0:T(8,128)S(1)}, u32[]{:S(2)}, u32[]{:S(2)}) collective-permute-start(f32[2,2,128,128]{3,2,1,0:T(8,128)S(1)} %get-tuple-element.62), channel_id=1, source_target_pairs={{1,2},{2,1},{3,4},{4,3},{5,6},{6,5},{7,8},{8,7},{9,10},{10,9},{11,... | collective-permute-start | bytes 786440 | tf_op jit(solution)/shard_map/ppermute | solution.py:428
  97.4 2.2 %all-gather.7 = f32[4,2,128,128]{3,2,1,0:T(8,128)S(1)} all-gather(f32[2,2,128,128]{3,2,1,0:T(8,128)S(1)} %get-tuple-element.61), channel_id=9, replica_groups={{0,1},{2,3},{4,5},{6,7},{8,9},{10,11},{12,13},{14,15},{16,17},{18,19},{..., dimensions={0}, use_global_device_ids=true | all-gather | bytes 786432 | tf_op jit(solution)/shard_map/all_gather | solution.py:433
  99.6 5.7 %collective-permute-done.8.far = f32[2,2,128,128]{3,2,1,0:T(8,128)S(1)} collective-permute-done((f32[2,2,128,128]{3,2,1,0:T(8,128)S(1)}, f32[2,2,128,128]{3,2,1,0:T(8,128)S(1)}, u32[]{:S(2)}, u32[]{:S(2)}) %collective-permute-start.8) | collective-permute-done | bytes 262176 | tf_op jit(solution)/shard_map/ppermute | solution.py:428
  105.9 1.9 %collective-permute-start.9 = (f32[2,256,128]{2,1,0:T(8,128)S(1)}, f32[2,256,128]{2,1,0:T(8,128)S(1)}, u32[]{:S(2)}, u32[]{:S(2)}) collective-permute-start(f32[2,256,128]{2,1,0:T(8,128)S(1)} %get-tuple-element.64), channel_id=1, source_target_pairs={{1,2},{2,1},{3,4},{4,3},{5,6},{6,5},{7,8},{8,7},{9,10},{10,9},{11,... | collective-permute-start | bytes 786440 | tf_op jit(solution)/shard_map/ppermute | solution.py:428
  107.8 5.1 %collective-permute-start.10 = (f32[2,2,128,128]{3,2,1,0:T(8,128)S(1)}, f32[2,2,128,128]{3,2,1,0:T(8,128)S(1)}, u32[]{:S(2)}, u32[]{:S(2)}) collective-permute-start(f32[2,2,128,128]{3,2,1,0:T(8,128)S(1)} %get-tuple-element.65), channel_id=1, source_target_pairs={{0,16},{16,0},{32,48},{48,32},{64,80},{80,64},{96,112},{112,96},{1... | collective-permute-start | bytes 786440 | tf_op jit(solution)/shard_map/ppermute | solution.py:428
  113.0 1.9 %collective-permute-start.11 = (f32[2,2,128,128]{3,2,1,0:T(8,128)S(1)}, f32[2,2,128,128]{3,2,1,0:T(8,128)S(1)}, u32[]{:S(2)}, u32[]{:S(2)}) collective-permute-start(f32[2,2,128,128]{3,2,1,0:T(8,128)S(1)} %get-tuple-element.66), channel_id=1, source_target_pairs={{16,32},{32,16},{48,64},{64,48},{80,96},{96,80},{17,33},{33,17},{4... | collective-permute-start | bytes 786440 | tf_op jit(solution)/shard_map/ppermute | solution.py:428
  114.9 2.2 %all-gather.6 = f32[4,256,128]{2,1,0:T(8,128)S(1)} all-gather(f32[2,256,128]{2,1,0:T(8,128)S(1)} %get-tuple-element.60), channel_id=8, replica_groups={{0,1},{2,3},{4,5},{6,7},{8,9},{10,11},{12,13},{14,15},{16,17},{18,19},{..., dimensions={0}, use_global_device_ids=true | all-gather | bytes 786432 | tf_op jit(solution)/shard_map/all_gather | solution.py:433
  118.2 1.8 %collective-permute-done.10.halo_a = f32[2,2,128,128]{3,2,1,0:T(8,128)S(1)} collective-permute-done((f32[2,2,128,128]{3,2,1,0:T(8,128)S(1)}, f32[2,2,128,128]{3,2,1,0:T(8,128)S(1)}, u32[]{:S(2)}, u32[]{:S(2)}) %collective-permute-start.10) | collective-permute-done | bytes 262176 | tf_op jit(solution)/shard_map/ppermute | solution.py:428
  120.0 3.6 %collective-permute-done.11.halo_b = f32[2,2,128,128]{3,2,1,0:T(8,128)S(1)} collective-permute-done((f32[2,2,128,128]{3,2,1,0:T(8,128)S(1)}, f32[2,2,128,128]{3,2,1,0:T(8,128)S(1)}, u32[]{:S(2)}, u32[]{:S(2)}) %collective-permute-start.11) | collective-permute-done | bytes 262176 | tf_op jit(solution)/shard_map/ppermute | solution.py:428
  123.6 1.5 %shard_map.126 = f32[2,256,256]{2,1,0:T(8,128)} custom-call(s32[4]{0:T(128)S(1)} %pad_add_fusion.info, f32[512,128]{1,0:T(8,128)S(1)} %get-tuple-element.55.ext_r, f32[512,128]{1,0:T(8,128)S(1)} %get-tuple-element.56.ext_i, f32[2,512,128]{2,1,0:T(8,128)S(1)} %get-tuple-element.57.ext_b, f32[2,512,128]{2,1,0:T(8,128)S(1)} %get-tuple-element.58.inner_a, ...), custom_call_target="tpu_custom_call" | custom-call | flops 1048576 | bytes 8388608 | tf_op jit(solution)/shard_map/pallas_call | solution.py:48
  (33 shorter events, 9.8 us)
Async XLA Ops:
  0.1 1.0 copy-start
  1.7 18.8 %copy-start.1 = (f32[2,256,256]{2,1,0:T(8,128)S(1)}, f32[2,256,256]{2,1,0:T(8,128)}, u32[]{:S(2)}) copy-start(f32[2,256,256]{2,1,0:T(8,128)} %tile.3) | copy-start | bytes 1572868
  1.8 18.8 %collective-permute-start = (f32[2,128,256]{2,1,0:T(8,128)S(1)}, f32[2,128,256]{2,1,0:T(8,128)S(1)}, u32[]{:S(2)}, u32[]{:S(2)}) collective-permute-start(f32[2,128,256]{2,1,0:T(8,128)S(1)} %get-tuple-element.36), channel_id=1, source_target_pairs={{0,16},{16,0},{32,48},{48,32},{64,80},{80,64},{96,112},{112,96},{1... | collective-permute-start | bytes 786440 | tf_op jit(solution)/shard_map/ppermute | solution.py:428
  4.0 16.6 %collective-permute-start.1 = (f32[2,128,256]{2,1,0:T(8,128)S(1)}, f32[2,128,256]{2,1,0:T(8,128)S(1)}, u32[]{:S(2)}, u32[]{:S(2)}) collective-permute-start(f32[2,128,256]{2,1,0:T(8,128)S(1)} %get-tuple-element.37), channel_id=1, source_target_pairs={{16,32},{32,16},{48,64},{64,48},{80,96},{96,80},{17,33},{33,17},{4... | collective-permute-start | bytes 786440 | tf_op jit(solution)/shard_map/ppermute | solution.py:428
  7.2 21.3 %collective-permute-start.2 = (f32[2,256,128]{2,1,0:T(8,128)S(1)}, f32[2,256,128]{2,1,0:T(8,128)S(1)}, u32[]{:S(2)}, u32[]{:S(2)}) collective-permute-start(f32[2,256,128]{2,1,0:T(8,128)S(1)} %get-tuple-element.43), channel_id=1, source_target_pairs={{1,2},{2,1},{3,4},{4,3},{5,6},{6,5},{7,8},{8,7},{9,10},{10,9},{11,... | collective-permute-start | bytes 786440 | tf_op jit(solution)/shard_map/ppermute | solution.py:428
  13.4 1.4 %copy-start.2 = (s32[1,1,6,256,256]{4,3,2,1,0:T(8,128)S(1)}, s32[1,1,6,256,256]{4,3,2,1,0:T(8,128)}, u32[]{:S(2)}) copy-start(s32[1,1,6,256,256]{4,3,2,1,0:T(8,128)} %param.16) | copy-start | bytes 4718596
  14.8 1.0 copy-start.3
  15.8 0.9 copy-start.9
  20.5 10.6 %copy-start.4 = (bf16[768,256]{1,0:T(8,128)(2,1)S(1)}, bf16[768,256]{1,0:T(8,128)(2,1)}, u32[]{:S(2)}) copy-start(bf16[768,256]{1,0:T(8,128)(2,1)} %constant.46.clone.refs_9_.refs_8_) | copy-start | bytes 1179652
  20.5 10.6 %copy-start.5 = (bf16[256,768]{1,0:T(8,128)(2,1)S(1)}, bf16[256,768]{1,0:T(8,128)(2,1)}, u32[]{:S(2)}) copy-start(bf16[256,768]{1,0:T(8,128)(2,1)} %constant.45.clone.refs_7_.refs_6_) | copy-start | bytes 1179652
  20.5 10.6 %copy-start.6 = (bf16[256,768]{1,0:T(8,128)(2,1)S(1)}, bf16[256,768]{1,0:T(8,128)(2,1)}, u32[]{:S(2)}) copy-start(bf16[256,768]{1,0:T(8,128)(2,1)} %constant.44.clone.refs_8_.refs_7_) | copy-start | bytes 1179652
  20.5 10.6 %copy-start.7 = (bf16[768,256]{1,0:T(8,128)(2,1)S(1)}, bf16[768,256]{1,0:T(8,128)(2,1)}, u32[]{:S(2)}) copy-start(bf16[768,256]{1,0:T(8,128)(2,1)} %constant.43.clone.refs_6_.refs_5_) | copy-start | bytes 1179652
  20.5 10.5 %copy-start.8 = (f32[2,128,256]{2,1,0:T(8,128)S(1)}, f32[2,128,256]{2,1,0:T(8,128)}, u32[]{:S(2)}) copy-start(f32[2,128,256]{2,1,0:T(8,128)} %constant.48.clone.refs_11_.refs_10_) | copy-start | bytes 786436
  20.5 10.5 %copy-start.10 = (f32[2,1,128]{2,1,0:T(1,128)S(1)}, f32[2,1,128]{2,1,0:T(1,128)}, u32[]{:S(2)}) copy-start(f32[2,1,128]{2,1,0:T(1,128)} %constant.47.clone.refs_10_.refs_9_) | copy-start | bytes 3076
  21.3 9.8 %collective-permute-start.3 = (f32[2,2,128,128]{3,2,1,0:T(8,128)S(1)}, f32[2,2,128,128]{3,2,1,0:T(8,128)S(1)}, u32[]{:S(2)}, u32[]{:S(2)}) collective-permute-start(f32[2,2,128,128]{3,2,1,0:T(8,128)S(1)} %get-tuple-element.44), channel_id=1, source_target_pairs={{1,2},{2,1},{3,4},{4,3},{5,6},{6,5},{7,8},{8,7},{9,10},{10,9},{11,... | collective-permute-start | bytes 786440 | tf_op jit(solution)/shard_map/ppermute | solution.py:428
  39.3 12.6 %collective-permute-start.4 = (f32[2,512,128]{2,1,0:T(8,128)S(1)}, f32[2,512,128]{2,1,0:T(8,128)S(1)}, u32[]{:S(2)}, u32[]{:S(2)}) collective-permute-start(f32[2,512,128]{2,1,0:T(8,128)S(1)} %get-tuple-element.51), channel_id=1, source_target_pairs={{1,2},{2,1},{3,4},{4,3},{5,6},{6,5},{7,8},{8,7},{9,10},{10,9},{11,... | collective-permute-start | bytes 1572872 | tf_op jit(solution)/shard_map/ppermute | solution.py:428
  52.7 16.3 %collective-permute-start.5 = (f32[2,2,256,128]{3,2,1,0:T(8,128)S(1)}, f32[2,2,256,128]{3,2,1,0:T(8,128)S(1)}, u32[]{:S(2)}, u32[]{:S(2)}) collective-permute-start(f32[2,2,256,128]{3,2,1,0:T(8,128)S(1)} %get-tuple-element.53), channel_id=1, source_target_pairs={{0,16},{16,0},{32,48},{48,32},{64,80},{80,64},{96,112},{112,96},{1... | collective-permute-start | bytes 1572872 | tf_op jit(solution)/shard_map/ppermute | solution.py:428
  56.3 16.3 %collective-permute-start.6 = (f32[2,2,256,128]{3,2,1,0:T(8,128)S(1)}, f32[2,2,256,128]{3,2,1,0:T(8,128)S(1)}, u32[]{:S(2)}, u32[]{:S(2)}) collective-permute-start(f32[2,2,256,128]{3,2,1,0:T(8,128)S(1)} %get-tuple-element.54), channel_id=1, source_target_pairs={{16,32},{32,16},{48,64},{64,48},{80,96},{96,80},{17,33},{33,17},{4... | collective-permute-start | bytes 1572872 | tf_op jit(solution)/shard_map/ppermute | solution.py:428
  73.5 13.8 %collective-permute-start.7 = (f32[2,512,128]{2,1,0:T(8,128)S(1)}, f32[2,512,128]{2,1,0:T(8,128)S(1)}, u32[]{:S(2)}, u32[]{:S(2)}) collective-permute-start(f32[2,512,128]{2,1,0:T(8,128)S(1)} %get-tuple-element.57.ext_b), channel_id=1, source_target_pairs={{1,2},{2,1},{3,4},{4,3},{5,6},{6,5},{7,8},{8,7},{9,10},{10,9},{11,... | collective-permute-start | bytes 1572872 | tf_op jit(solution)/shard_map/ppermute | solution.py:428
  95.5 9.8 %collective-permute-start.8 = (f32[2,2,128,128]{3,2,1,0:T(8,128)S(1)}, f32[2,2,128,128]{3,2,1,0:T(8,128)S(1)}, u32[]{:S(2)}, u32[]{:S(2)}) collective-permute-start(f32[2,2,128,128]{3,2,1,0:T(8,128)S(1)} %get-tuple-element.62), channel_id=1, source_target_pairs={{1,2},{2,1},{3,4},{4,3},{5,6},{6,5},{7,8},{8,7},{9,10},{10,9},{11,... | collective-permute-start | bytes 786440 | tf_op jit(solution)/shard_map/ppermute | solution.py:428
  105.9 12.3 %collective-permute-start.9 = (f32[2,256,128]{2,1,0:T(8,128)S(1)}, f32[2,256,128]{2,1,0:T(8,128)S(1)}, u32[]{:S(2)}, u32[]{:S(2)}) collective-permute-start(f32[2,256,128]{2,1,0:T(8,128)S(1)} %get-tuple-element.64), channel_id=1, source_target_pairs={{1,2},{2,1},{3,4},{4,3},{5,6},{6,5},{7,8},{8,7},{9,10},{10,9},{11,... | collective-permute-start | bytes 786440 | tf_op jit(solution)/shard_map/ppermute | solution.py:428
  107.8 12.2 %collective-permute-start.10 = (f32[2,2,128,128]{3,2,1,0:T(8,128)S(1)}, f32[2,2,128,128]{3,2,1,0:T(8,128)S(1)}, u32[]{:S(2)}, u32[]{:S(2)}) collective-permute-start(f32[2,2,128,128]{3,2,1,0:T(8,128)S(1)} %get-tuple-element.65), channel_id=1, source_target_pairs={{0,16},{16,0},{32,48},{48,32},{64,80},{80,64},{96,112},{112,96},{1... | collective-permute-start | bytes 786440 | tf_op jit(solution)/shard_map/ppermute | solution.py:428
  113.0 10.7 %collective-permute-start.11 = (f32[2,2,128,128]{3,2,1,0:T(8,128)S(1)}, f32[2,2,128,128]{3,2,1,0:T(8,128)S(1)}, u32[]{:S(2)}, u32[]{:S(2)}) collective-permute-start(f32[2,2,128,128]{3,2,1,0:T(8,128)S(1)} %get-tuple-element.66), channel_id=1, source_target_pairs={{16,32},{32,16},{48,64},{64,48},{80,96},{96,80},{17,33},{33,17},{4... | collective-permute-start | bytes 786440 | tf_op jit(solution)/shard_map/ppermute | solution.py:428
